TPU v7x, 32 devices: a whole 2x2x4 slice. The times are simulated.
32 devices in a mesh: groups: 2 (over y), tile: 4 (over z), chan: 2 (over x), tm: 2 (over core).
Axes of the slice: x: 2, y: 2, z: 4, core: 2. Of those that a mesh axis runs over, the one named last changes fastest.
Arguments:
- latents: bfloat16 [8, 32, 576], P('tm', 'groups', 'tile'), parts along dimension 1, may hold values from -6 to 6
- tile_order: int32 [8], P('groups'), parts along dimension 0, may hold values from 0 to 3, each once
- w_in: bfloat16 [27, 16, 512], P(None, None, 'chan'), may hold values from -0.3125 to 0.3125
- gain_in: float32 [512], P('chan'), may hold values from 0.25 to 1.75
- shift_in: float32 [512], P('chan'), may hold values from -3 to 3
- w_mid: bfloat16 [27, 512, 512], P(None, None, 'chan'), may hold values from -0.0546875 to 0.0546875
- gain_mid: float32 [512], P('chan'), may hold values from 0.25 to 1.75
- shift_mid: float32 [512], P('chan'), may hold values from -3 to 3
- w_out: bfloat16 [3, 512], P(None, 'chan'), may hold values from -0.25 to 0.25
- blend_weight: float32 [8, 256], P('groups'), parts along dimension 0, may hold values from 0.25 to 4
Outputs:
- decoded: float32 [8, 6, 576], P('tm', 'groups', 'tile'), parts along dimension 1
There are 2 independent parts, one for each index of `groups`. A program takes and returns all parts, laid end to end along the dimension named above; an argument that names none is the same for every part. Nothing has to cross between parts.
Inputs may be any that keep to these rules, and one draw needn't show every extreme that they name: `tile_order`: each image block is held by exactly one latent block.
All inputs are finite; a program needn't handle non-finite values.
Results may differ from a plain program's by a relative error of at most 0.0037.
Values may be sent and summed in bfloat16 or wider, within the bound.
A program may use at most 64 MiB of HBM per device.

v0:
```python
import jax
import jax.numpy as jnp
from jax import lax
from jax.sharding import PartitionSpec as P

CH = 512
GROUPS = 32
TSIDE = 16
STRIDE = 12
GRID_X = 4


EPSILON = 1e-06


def shifted(value, axis, steps):
    count = lax.axis_size(axis)
    leading, last = (max(0, -steps), min(count, count - steps))
    return lax.ppermute(value, axis, [(source, source + steps) for source in range(leading, last)])


def window_index(tile_id, tiles):
    slots = jnp.arange(TSIDE * TSIDE, dtype=jnp.int32)
    row = tile_id // GRID_X * STRIDE + slots // TSIDE
    col = tile_id % GRID_X * STRIDE + slots % TSIDE
    valid = (row < tiles // GRID_X * STRIDE) & (col < GRID_X * STRIDE)
    block = row // STRIDE * GRID_X + col // STRIDE
    index = block * (STRIDE * STRIDE) + row % STRIDE * STRIDE + col % STRIDE
    return (jnp.where(valid, index, 0), valid)


def causal_conv(extended, weights, frames, side):
    pixels = side * side
    rows = jnp.arange(pixels, dtype=jnp.int32) // side
    cols = jnp.arange(pixels, dtype=jnp.int32) % side
    total = jnp.zeros((frames, weights.shape[2], pixels), jnp.float32)
    for depth in range(3):
        window = extended[depth : depth + frames]
        for down in range(3):
            for across in range(3):
                offset = (down - 1) * side + (across - 1)
                inside = (
                    (rows + down - 1 >= 0)
                    & (rows + down - 1 < side)
                    & (cols + across - 1 >= 0)
                    & (cols + across - 1 < side)
                )
                moved = jnp.roll(window, -offset, axis=2)
                moved = jnp.where(inside[None, None, :], moved, jnp.zeros_like(moved))
                total = total + jnp.einsum(
                    "fcp,co->fop",
                    moved,
                    weights[9 * depth + 3 * down + across],
                    preferred_element_type=jnp.float32,
                )
    return total


def with_history(values):
    frames = values.shape[0]
    earlier = shifted(values[frames - 2 :], "tm", 1)
    return jnp.concatenate([earlier, values], axis=0)


def normalize(values, gain, shift, total_frames):
    frames, chans, pixels = values.shape
    width = CH // GROUPS
    grouped = values.reshape(frames, chans // width, width, pixels)
    sums = jnp.sum(grouped, axis=(0, 2, 3))
    squares = jnp.sum(grouped * grouped, axis=(0, 2, 3))
    sums, squares = lax.psum((sums, squares), "tm")
    count = total_frames * width * pixels
    mean = sums / count
    variance = squares / count - mean * mean
    scale = lax.rsqrt(variance + EPSILON)
    normed = (grouped - mean[None, :, None, None]) * scale[None, :, None, None]
    normed = normed.reshape(frames, chans, pixels) * gain[None, :, None] + shift[None, :, None]
    return jax.nn.silu(normed).astype(jnp.bfloat16)


def spread(color, weight, index, total_pixels):
    numer = (
        jnp.zeros((color.shape[0], 3, total_pixels), jnp.float32)
        .at[:, :, index]
        .add(color * weight[None, None, :])
    )
    denom = jnp.zeros((total_pixels,), jnp.float32).at[index].add(weight)
    return (numer, denom)


def route_owned(numer, denom, tile_id, own):
    frames = numer.shape[0]
    margin = (GRID_X + 1) * own
    numer_wide = jnp.concatenate([numer, jnp.zeros((frames, 3, margin), jnp.float32)], axis=2)
    denom_wide = jnp.concatenate([denom, jnp.zeros((margin,), jnp.float32)], axis=0)
    first_pixel = tile_id * own

    def block_at(offset):
        start_pixel = first_pixel + offset * own
        return (
            lax.dynamic_slice_in_dim(numer_wide, start_pixel, own, 2),
            lax.dynamic_slice_in_dim(denom_wide, start_pixel, own, 0),
        )

    owned_numer, owned_denom = block_at(0)
    for offset in (1, GRID_X, GRID_X + 1):
        piece_numer, piece_denom = block_at(offset)
        got_numer, got_denom = shifted((piece_numer, piece_denom), "tile", offset)
        owned_numer = owned_numer + got_numer
        owned_denom = owned_denom + got_denom
    return (owned_numer, owned_denom)


def body(
    latents, tile_order, w_in, gain_in, shift_in, w_mid, gain_mid, shift_mid, w_out, blend_weight
):
    frames = latents.shape[0]
    total_frames = frames * lax.axis_size("tm")
    tiles = tile_order.shape[0]
    own = STRIDE * STRIDE
    total_pixels = tiles * own
    tile_id = lax.axis_index("tile")
    index, valid = window_index(tile_id, tiles)
    whole = lax.all_gather(latents, "tile", axis=2, tiled=True)
    blocks = whole.reshape(frames, whole.shape[1], tiles, own)
    image = (
        jnp.zeros_like(blocks)
        .at[:, :, tile_order]
        .set(blocks)
        .reshape(frames, whole.shape[1], total_pixels)
    )
    window = jnp.where(
        valid[None, None, :], jnp.take(image, index, axis=2), jnp.zeros((), jnp.bfloat16)
    )
    first = causal_conv(with_history(window), w_in, frames, TSIDE)
    hidden = normalize(first, gain_in, shift_in, total_frames)
    second = causal_conv(
        lax.all_gather(with_history(hidden), "chan", axis=1, tiled=True), w_mid, frames, TSIDE
    )
    upper = normalize(second, gain_mid, shift_mid, total_frames)
    color = jnp.einsum("oc,fcp->fop", w_out, upper, preferred_element_type=jnp.float32)
    weight = jnp.where(valid, blend_weight[tile_id], jnp.float32(0.0))
    numer, denom = spread(color, weight, index, total_pixels)
    numer, denom = route_owned(numer, denom, tile_id, own)
    numer = lax.psum(numer, "chan")
    return numer / denom[None, None, :]


def solution(mesh):
    placed = (
        P("tm", "groups", "tile"),
        P("groups"),
        P(None, None, "chan"),
        P("chan"),
        P("chan"),
        P(None, None, "chan"),
        P("chan"),
        P("chan"),
        P(None, "chan"),
        P("groups", None),
    )
    return jax.shard_map(
        body, mesh=mesh, in_specs=placed, out_specs=P("tm", "groups", "tile"), check_vma=False
    )
```

profile of v0, /device:TPU:0, one launch (start us, length us, event | category | flops | bytes accessed | tf_op | source)
XLA Modules:
  0.0 141.7 jit_solution(11770328538480830236)
XLA Ops:
  6.6 1.0 copy.204
  7.6 18.3 %all_gather.6 = bf16[4,16,576]{1,0,2:T(4,128)(2,1)S(1)} all-gather(bf16[4,16,144]{1,0,2:T(4,128)(2,1)S(1)} %copy.204), channel_id=1, replica_groups=mesh['groups'=2,'tile'=4,'chan'=2,'tm'=2] {'tile'}, dimensions={2}, use_global_device_ids=true | all-gather | bytes 92160 | tf_op jit(solution)/shard_map/all_gather | solution.py:124
  26.2 0.7 compare_select_fusion.2
  26.9 0.7 scatter_fusion
  27.9 1.0 gather_fusion
  29.1 1.3 collective-permute-start
  30.5 0.7 collective-permute-done
  31.4 0.4 fusion.206
  33.3 0.4 convolution_add_fusion.13
  36.1 0.4 convolution_add_fusion.6
  36.5 0.4 convolution_add_fusion.5
  36.9 0.4 convolution_add_fusion.4
  39.3 0.4 fusion.8
  39.7 0.4 fusion.7
  40.2 0.4 fusion.6
  42.6 0.4 fusion.503
  43.4 2.5 %all-reduce.3 = (f32[16]{0:T(128)S(1)}, f32[16]{0:T(128)S(1)}) all-reduce(f32[16]{0:T(128)S(1)} %reduce_sum.54, f32[16]{0:T(128)S(1)} %reduce_sum.51), channel_id=1, replica_groups=mesh['groups'=2,'tile'=4,'chan'=2,'tm'=2] {'tm'}, use_global_device_ids=true, to_apply=%region_6.7 | all-reduce | flops 32 | bytes 256 | tf_op jit(solution)/shard_map/psum | solution.py:71
  46.6 2.3 %collective-permute-start.1 = (bf16[2,256,256]{1,2,0:T(8,128)(2,1)S(1)}, bf16[2,256,256]{1,2,0:T(8,128)(2,1)S(1)}, u32[]{:S(2)}, u32[]{:S(2)}) collective-permute-start(bf16[2,256,256]{1,2,0:T(8,128)(2,1)S(1)} %slice.825), channel_id=1, source_target_pairs={{0,1},{2,3},{4,5},{6,7},{8,9},{10,11},{12,13},{14,15},{16,17},{18,... | collective-permute-start | bytes 786440 | tf_op jit(solution)/shard_map/ppermute | solution.py:19
  48.9 1.1 collective-permute-done.1
  50.0 0.9 pad_maximum_fusion
  51.0 2.3 %scatter_custom_fusion.2 = f32[576]{0:T(1024)S(1)} fusion(s32[256]{0:T(256)S(1)} %bitcast.322, f32[256]{0:T(256)S(1)} %broadcast_select_fusion, f32[]{:T(128)} %constant.166.clone.1), kind=kCustom, calls=%fused_computation.579 | custom fusion | flops 256 | bytes 2308 | tf_op jit(solution)/shard_map/scatter-add | solution.py:87
  53.4 3.4 %collective-permute-start.5 = (f32[144]{0:T(256)S(1)}, f32[144]{0:T(256)S(1)}, u32[]{:S(2)}, u32[]{:S(2)}) collective-permute-start(f32[144]{0:T(256)S(1)} %get-tuple-element.115), channel_id=1, source_target_pairs={{0,4},{4,8},{8,12},{1,5},{5,9},{9,13},{2,6},{6,10},{10,14},{3,7},{... | collective-permute-start | bytes 1736 | tf_op jit(solution)/shard_map/ppermute | solution.py:19
  56.9 0.7 collective-permute-start.6
  57.5 0.8 collective-permute-start.7
  58.4 21.1 %all-gather.2.cloned.1.call-done = bf16[6,512,256]{1,2,0:T(8,128)(2,1)} async-done(((bf16[6,256,256]{1,2,0:T(8,128)(2,1)}), bf16[6,512,256]{1,2,0:T(8,128)(2,1)}) %all-gather.2.cloned.1.call-update) | async-done | bytes 1572880 | tf_op jit(solution)/shard_map/all_gather | solution.py:138
  79.5 4.2 %fusion.506 = (bf16[4,512,239]{1,2,0:T(8,128)(2,1)S(1)}, bf16[4,512,239]{1,2,0:T(8,128)(2,1)S(1)}, bf16[4,512,239]{1,2,0:T(8,128)(2,1)S(1)}, bf16[4,512,239]{1,2...) fusion(bf16[6,512,256]{1,2,0:T(8,128)(2,1)} %all-gather.2.cloned.1.call-done), kind=kLoop, calls=%fused_computation.741 | loop fusion | bytes 11747328 | tf_op jit(solution)/shard_map/jit(_roll_static)/slice | solution.py:48
  83.8 1.4 %fusion.23 = f32[4,256,256]{2,1,0:T(8,128)S(1)} fusion(bf16[4,512,239]{1,2,0:T(8,128)(2,1)S(1)} %get-tuple-element.30, bf16[4,512,17]{1,2,0:T(8,128)(2,1)S(1)} %get-tuple-element.36, pred[256]{0:T(512)(128)(4,1)S(1)} %and_and_fusion.8, bf16[27,512,256]{2,1,0:T(8,128)(2,1)} %param.15), kind=kOutput, calls=%fused_computation.84 | convolution fusion | flops 271056896 | bytes 2359552 | tf_op jit(solution)/shard_map/fcp,co->fop/dot_general | solution.py:50
  85.2 1.4 %convolution_bitcast_fusion.8 = f32[4,256,256]{1,2,0:T(8,128)S(1)} fusion(bf16[4,512,239]{1,2,0:T(8,128)(2,1)S(1)} %get-tuple-element.27, bf16[4,512,17]{1,2,0:T(8,128)(2,1)S(1)} %get-tuple-element.33, pred[256]{0:T(512)(128)(4,1)S(1)} %and_and_fusion.8, bf16[27,512,256]{2,1,0:T(8,128)(2,1)} %param.15), kind=kOutput, calls=%fused_computation.12 | convolution fusion | flops 271056896 | bytes 2359552 | tf_op jit(solution)/shard_map/fcp,co->fop/dot_general | solution.py:50
  86.7 0.7 fusion.508
  87.4 1.4 %convolution_bitcast_fusion.7 = f32[4,256,256]{1,2,0:T(8,128)S(1)} fusion(bf16[4,512,240]{1,2,0:T(8,128)(2,1)S(1)} %get-tuple-element.39, bf16[4,512,16]{1,2,0:T(8,128)(2,1)S(1)} %get-tuple-element.45, pred[256]{0:T(512)(128)(4,1)S(1)} %get-tuple-element.131, bf16[27,512,256]{2,1,0:T(8,128)(2,1)} %param.15), kind=kOutput, calls=%fused_computation.11 | convolution fusion | flops 271056896 | bytes 2359552 | tf_op jit(solution)/shard_map/fcp,co->fop/dot_general | solution.py:50
  88.8 0.7 fusion.510
  89.6 1.5 %convolution_bitcast_fusion.6 = f32[4,256,256]{1,2,0:T(8,128)S(1)} fusion(bf16[4,512,241]{1,2,0:T(8,128)(2,1)S(1)} %get-tuple-element.51, bf16[4,512,15]{1,2,0:T(8,128)(2,1)S(1)} %get-tuple-element.57, pred[256]{0:T(512)(128)(4,1)S(1)} %get-tuple-element.130, bf16[27,512,256]{2,1,0:T(8,128)(2,1)} %param.15), kind=kOutput, calls=%fused_computation.10 | convolution fusion | flops 271056896 | bytes 2359552 | tf_op jit(solution)/shard_map/fcp,co->fop/dot_general | solution.py:50
  91.0 0.8 fusion.504
  91.9 1.4 %convolution_bitcast_fusion.5 = f32[4,256,256]{1,2,0:T(8,128)S(1)} fusion(bf16[4,512,255]{1,2,0:T(8,128)(2,1)S(1)} %get-tuple-element.14, bf16[4,512,1]{1,2,0:T(2,128)(2,1)S(1)} %get-tuple-element.20, pred[256]{0:T(512)(128)(4,1)S(1)} %get-tuple-element.129, bf16[27,512,256]{2,1,0:T(8,128)(2,1)} %param.15), kind=kOutput, calls=%fused_computation.9 | convolution fusion | flops 271056896 | bytes 2359552 | tf_op jit(solution)/shard_map/fcp,co->fop/dot_general | solution.py:50
  93.4 1.6 %convolution_bitcast_fusion.2 = f32[4,256,256]{1,2,0:T(8,128)S(1)} fusion(bf16[4,512,15]{1,2,0:T(8,128)(2,1)S(1)} %get-tuple-element.56, bf16[4,512,241]{1,2,0:T(8,128)(2,1)S(1)} %get-tuple-element.50, pred[256]{0:T(512)(128)(4,1)S(1)} %get-tuple-element.126, bf16[27,512,256]{2,1,0:T(8,128)(2,1)} %param.15), kind=kOutput, calls=%fused_computation.6 | convolution fusion | flops 271056896 | bytes 2359552 | tf_op jit(solution)/shard_map/fcp,co->fop/dot_general | solution.py:50
  95.0 1.4 %convolution_bitcast_fusion.1 = f32[4,256,256]{1,2,0:T(8,128)S(1)} fusion(bf16[4,512,16]{1,2,0:T(8,128)(2,1)S(1)} %get-tuple-element.44, bf16[4,512,240]{1,2,0:T(8,128)(2,1)S(1)} %get-tuple-element.38, pred[256]{0:T(512)(128)(4,1)S(1)} %get-tuple-element.125, bf16[27,512,256]{2,1,0:T(8,128)(2,1)} %param.15), kind=kOutput, calls=%fused_computation.5 | convolution fusion | flops 271056896 | bytes 2359552 | tf_op jit(solution)/shard_map/fcp,co->fop/dot_general | solution.py:50
  96.4 1.6 %convolution_bitcast_fusion = f32[4,256,256]{1,2,0:T(8,128)S(1)} fusion(bf16[4,512,17]{1,2,0:T(8,128)(2,1)S(1)} %get-tuple-element.32, bf16[4,512,239]{1,2,0:T(8,128)(2,1)S(1)} %get-tuple-element.26, pred[256]{0:T(512)(128)(4,1)S(1)} %get-tuple-element.124, bf16[27,512,256]{2,1,0:T(8,128)(2,1)} %param.15), kind=kOutput, calls=%fused_computation.4 | convolution fusion | flops 271056896 | bytes 2359552 | tf_op jit(solution)/shard_map/fcp,co->fop/dot_general | solution.py:50
  98.0 1.5 %convolution_add_fusion.31 = f32[4,256,256]{2,1,0:T(8,128)S(1)} fusion(f32[4,256,256]{2,1,0:T(8,128)S(1)} %fusion.23, bf16[4,512,240]{1,2,0:T(8,128)(2,1)S(1)} %get-tuple-element.42, bf16[4,512,16]{1,2,0:T(8,128)(2,1)S(1)} %get-tuple-element.48, pred[256]{0:T(512)(128)(4,1)S(1)} %get-tuple-element.131, bf16[27,512,256]{2,1,0:T(8,128)(2,1)} %param.15), kind=kOutput, calls=%fused_computation.77 | convolution fusion | flops 271319040 | bytes 3408128 | tf_op jit(solution)/shard_map/fcp,co->fop/dot_general | solution.py:50
  99.5 0.5 convolution_add_fusion.30
  100.0 0.5 convolution_add_fusion.29
  100.5 0.5 convolution_add_fusion.28
  101.0 0.5 convolution_add_fusion.27
  101.5 0.5 convolution_add_fusion.26
  102.0 0.5 convolution_add_fusion.25
  102.5 0.5 convolution_add_fusion.24
  103.0 0.5 convolution_add_fusion.23
  103.5 0.5 convolution_add_fusion.22
  104.0 0.5 convolution_add_fusion.21
  104.5 0.5 convolution_add_fusion.20
  105.0 0.5 convolution_add_fusion.19
  105.5 0.5 convolution_add_fusion.18
  106.0 0.7 convolution_add_fusion.17
  106.7 0.5 fusion.21
  107.3 0.5 convolution_bitcast_fusion.4
  107.7 0.6 fusion.16
  108.4 0.6 fusion.502
  109.4 2.5 %all-reduce.2 = (f32[16]{0:T(128)S(1)}, f32[16]{0:T(128)S(1)}) all-reduce(f32[16]{0:T(128)S(1)} %reduce_sum.75, f32[16]{0:T(128)S(1)} %reduce_sum.72), channel_id=1, replica_groups=mesh['groups'=2,'tile'=4,'chan'=2,'tm'=2] {'tm'}, use_global_device_ids=true, to_apply=%region_12.13 | all-reduce | flops 32 | bytes 256 | tf_op jit(solution)/shard_map/psum | solution.py:71
  112.2 0.5 fusion.22
  113.1 8.5 %scatter_fusion.1 = f32[4,3,576]{1,0,2:T(4,128)S(1)} fusion(f32[4,3,576]{1,0,2:T(4,128)S(1)} %broadcast_in_dim.385, s32[256]{0:T(256)S(1)} %bitcast.323, f32[256,4,3]{2,1,0:T(4,128)S(1)} %copy.210), kind=kCustom, calls=%fused_computation.2 | custom fusion | flops 3072 | bytes 37888 | tf_op jit(solution)/shard_map/scatter-add | solution.py:85
  122.2 3.4 %collective-permute-start.2 = (f32[4,3,144]{2,0,1:T(4,128)S(1)}, f32[4,3,144]{2,0,1:T(4,128)S(1)}, u32[]{:S(2)}, u32[]{:S(2)}) collective-permute-start(f32[4,3,144]{2,0,1:T(4,128)S(1)} %get-tuple-element.112), channel_id=1, source_target_pairs={{0,4},{4,8},{8,12},{1,5},{5,9},{9,13},{2,6},{6,10},{10,14},{3,7},{... | collective-permute-start | bytes 20744 | tf_op jit(solution)/shard_map/ppermute | solution.py:19
  125.6 0.7 collective-permute-start.3
  126.2 0.7 collective-permute-start.4
  127.1 7.1 %psum.39 = f32[4,3,144]{2,0,1:T(4,128)S(1)} all-reduce(f32[4,3,144]{2,0,1:T(4,128)S(1)} %fusion.326), channel_id=1, replica_groups=mesh['groups'=2,'tile'=4,'chan'=2,'tm'=2] {'chan'}, use_global_device_ids=true, to_apply=%region_14.15 | all-reduce | flops 1728 | bytes 13824 | tf_op jit(solution)/shard_map/psum | solution.py:145
  134.2 0.6 broadcast_divide_fusion
  (104 shorter events, 11.9 us)
Async XLA Ops:
  6.5 44.4 %copy-start = (f32[4,256]{1,0:T(4,128)S(1)}, f32[4,256]{1,0:T(4,128)}, u32[]{:S(2)}) copy-start(f32[4,256]{1,0:T(4,128)} %param.19) | copy-start | bytes 12292
  6.5 24.9 %copy-start.3 = (bf16[27,16,256]{2,1,0:T(8,128)(2,1)S(1)}, bf16[27,16,256]{2,1,0:T(8,128)(2,1)}, u32[]{:S(2)}) copy-start(bf16[27,16,256]{2,1,0:T(8,128)(2,1)} %param.12) | copy-start | bytes 663556
  6.5 72.9 %all-gather.2.cloned.1.call-start = ((), (), s32[]{:S(2)}) async-start(), calls=%async_computation | async-start | bytes 2359296 | tf_op jit(solution)/shard_map/all_gather | solution.py:138
  29.1 2.1 %collective-permute-start = (bf16[2,16,256]{2,1,0:T(8,128)(2,1)S(1)}, bf16[2,16,256]{2,1,0:T(8,128)(2,1)S(1)}, u32[]{:S(2)}, u32[]{:S(2)}) collective-permute-start(bf16[2,16,256]{2,1,0:T(8,128)(2,1)S(1)} %slice.742), channel_id=1, source_target_pairs={{0,1},{2,3},{4,5},{6,7},{8,9},{10,11},{12,13},{14,15},{16,17},{18,... | collective-permute-start | bytes 49160 | tf_op jit(solution)/shard_map/ppermute | solution.py:19
  42.2 4.1 %copy-start.4 = (f32[256]{0:T(256)S(1)}, f32[256]{0:T(256)}, u32[]{:S(2)}) copy-start(f32[256]{0:T(256)} %param.14) | copy-start | bytes 3076
  42.2 4.0 %copy-start.5 = (f32[256]{0:T(256)S(1)}, f32[256]{0:T(256)}, u32[]{:S(2)}) copy-start(f32[256]{0:T(256)} %param.13) | copy-start | bytes 3076
  46.6 3.4 %collective-permute-start.1 = (bf16[2,256,256]{1,2,0:T(8,128)(2,1)S(1)}, bf16[2,256,256]{1,2,0:T(8,128)(2,1)S(1)}, u32[]{:S(2)}, u32[]{:S(2)}) collective-permute-start(bf16[2,256,256]{1,2,0:T(8,128)(2,1)S(1)} %slice.825), channel_id=1, source_target_pairs={{0,1},{2,3},{4,5},{6,7},{8,9},{10,11},{12,13},{14,15},{16,17},{18,... | collective-permute-start | bytes 786440 | tf_op jit(solution)/shard_map/ppermute | solution.py:19
  53.4 72.8 %collective-permute-start.5 = (f32[144]{0:T(256)S(1)}, f32[144]{0:T(256)S(1)}, u32[]{:S(2)}, u32[]{:S(2)}) collective-permute-start(f32[144]{0:T(256)S(1)} %get-tuple-element.115), channel_id=1, source_target_pairs={{0,4},{4,8},{8,12},{1,5},{5,9},{9,13},{2,6},{6,10},{10,14},{3,7},{... | collective-permute-start | bytes 1736 | tf_op jit(solution)/shard_map/ppermute | solution.py:19
  56.9 70.0 %collective-permute-start.6 = (f32[144]{0:T(256)S(1)}, f32[144]{0:T(256)S(1)}, u32[]{:S(2)}, u32[]{:S(2)}) collective-permute-start(f32[144]{0:T(256)S(1)} %get-tuple-element.116), channel_id=1, source_target_pairs={} | collective-permute-start | bytes 1736 | tf_op jit(solution)/shard_map/ppermute | solution.py:19
  57.5 69.4 %collective-permute-start.7 = (f32[144]{0:T(256)S(1)}, f32[144]{0:T(256)S(1)}, u32[]{:S(2)}, u32[]{:S(2)}) collective-permute-start(f32[144]{0:T(256)S(1)} %get-tuple-element.117), channel_id=1, source_target_pairs={} | collective-permute-start | bytes 1736 | tf_op jit(solution)/shard_map/ppermute | solution.py:19
  79.5 4.2 %copy-start.2 = (bf16[6,512,256]{1,2,0:T(8,128)(2,1)S(1)}, bf16[6,512,256]{1,2,0:T(8,128)(2,1)}, u32[]{:S(2)}) copy-start(bf16[6,512,256]{1,2,0:T(8,128)(2,1)} %all-gather.2.cloned.1.call-done) | copy-start | bytes 4718596
  93.4 6.1 %slice-start = ((s8[7077888]{0:T(1024)(128)(4,1)}), s8[4194304]{0:T(1024)(128)(4,1)S(1)}, s32[]{:S(2)}) async-start(s8[7077888]{0:T(1024)(128)(4,1)} %bitcast.319), calls=%async_computation.1 | async-start | bytes 8388608
  96.4 3.1 %slice-start.1 = ((s8[7077888]{0:T(1024)(128)(4,1)}), s8[2883584]{0:T(1024)(128)(4,1)S(1)}, s32[]{:S(2)}) async-start(s8[7077888]{0:T(1024)(128)(4,1)} %bitcast.319), calls=%async_computation.2 | async-start | bytes 5767168
  108.4 3.8 %copy-start.6 = (bf16[3,256]{1,0:T(4,128)(2,1)S(1)}, bf16[3,256]{1,0:T(4,128)(2,1)}, u32[]{:S(2)}) copy-start(bf16[3,256]{1,0:T(4,128)(2,1)} %param.18) | copy-start | bytes 4612
  108.4 3.8 %copy-start.7 = (f32[256]{0:T(256)S(1)}, f32[256]{0:T(256)}, u32[]{:S(2)}) copy-start(f32[256]{0:T(256)} %param.17) | copy-start | bytes 3076
  108.4 3.8 %copy-start.8 = (f32[256]{0:T(256)S(1)}, f32[256]{0:T(256)}, u32[]{:S(2)}) copy-start(f32[256]{0:T(256)} %param.16) | copy-start | bytes 3076
  112.7 22.2 %copy-start.1 = (f32[4,256]{1,0:T(4,128)S(1)}, f32[4,256]{1,0:T(4,128)}, u32[]{:S(2)}) copy-start(f32[4,256]{1,0:T(4,128)} %param.19) | copy-start | bytes 12292
  122.2 4.8 %collective-permute-start.2 = (f32[4,3,144]{2,0,1:T(4,128)S(1)}, f32[4,3,144]{2,0,1:T(4,128)S(1)}, u32[]{:S(2)}, u32[]{:S(2)}) collective-permute-start(f32[4,3,144]{2,0,1:T(4,128)S(1)} %get-tuple-element.112), channel_id=1, source_target_pairs={{0,4},{4,8},{8,12},{1,5},{5,9},{9,13},{2,6},{6,10},{10,14},{3,7},{... | collective-permute-start | bytes 20744 | tf_op jit(solution)/shard_map/ppermute | solution.py:19
  125.6 1.4 %collective-permute-start.3 = (f32[4,3,144]{2,0,1:T(4,128)S(1)}, f32[4,3,144]{2,0,1:T(4,128)S(1)}, u32[]{:S(2)}, u32[]{:S(2)}) collective-permute-start(f32[4,3,144]{2,0,1:T(4,128)S(1)} %get-tuple-element.113), channel_id=1, source_target_pairs={} | collective-permute-start | bytes 20744 | tf_op jit(solution)/shard_map/ppermute | solution.py:19
  126.2 0.8 collective-permute-start.4
Sparse Core Ops, SparseCore 0:
  51.1 28.3 all-gather.1
where the time goes:
time: 142 us
  matrix products  33.9 us (24%)
  blocking collectives  30.3 us (21%)
  waiting for transfers between devices  23 us (16%)
  other arithmetic  14.9 us (10%)
  between operations  14.3 us (10%)
  starting transfers between devices  13.2 us (9%)
  local copies, waits for them, and re-layouts  12.1 us (9%)
    dot_general x54, matrix products, causal_conv(): jnp.einsum('fcp,co->fop', moved, weights[9 * depth + 3 * down + across],...  33.5 us
    all_gather x1, waiting for transfers between devices, body(): lax.all_gather(with_history(hidden), 'chan', axis=1, tiled=True)  21.1 us
    all_gather x1, blocking collectives, body(): whole = lax.all_gather(latents, 'tile', axis=2, tiled=True)  18.3 us
    ppermute x8, starting transfers between devices, shifted(): lax.ppermute(value, axis, [(source, source + steps) for source in range(l...  13.2 us
    scatter-add x1, other arithmetic, spread(): numer = jnp.zeros((color.shape[0], 3, total_pixels), jnp.float32).at[:, :...  8.52 us
    psum x1, blocking collectives, body(): numer = lax.psum(numer, 'chan')  7.13 us
    slice x8, local copies, waits for them, and re-layouts, causal_conv(): moved = jnp.roll(window, -offset, axis=2)  6.55 us
    psum x2, blocking collectives, normalize(): sums, squares = lax.psum((sums, squares), 'tm')  4.95 us
  transfers between devices with their start and end apart: 9, of which 3 were waited for; matrix products, arithmetic and copies ran while one was open for 30% of the time, Pallas kernels for 0%

commit v1 on v0

v1 whole, which is shorter than its diff:
```python
import functools

import jax
import jax.numpy as jnp
from jax import lax
from jax.experimental import pallas as pl
from jax.experimental.pallas import tpu as pltpu
from jax.sharding import PartitionSpec as P

GROUPS = 32
TSIDE = 16
STRIDE = 12
GRID_X = 4
EPSILON = 1e-06
LANES = 128
MESH = pl.DeviceIdType.MESH


def place_matrix(down, across, kind):
    pixels = TSIDE * TSIDE
    pixel = lax.broadcasted_iota(jnp.int32, (2 * LANES, pixels), 0)
    slot = lax.broadcasted_iota(jnp.int32, (2 * LANES, pixels), 1)
    row = slot // TSIDE - STRIDE * down
    col = slot % TSIDE - STRIDE * across
    inside = (row >= 0) & (row < STRIDE) & (col >= 0) & (col < STRIDE)
    hit = inside & (pixel == row * STRIDE + col)
    return jnp.where(hit, 1.0, 0.0).astype(kind)


def group_sums(sums, squares, width):
    chans = sums.shape[1]
    chunks = chans // LANES
    rows = [v[:, LANES * i : LANES * (i + 1)] for v in (sums, squares) for i in range(chunks)]
    if len(rows) < 8:
        rows.append(jnp.zeros((8 - len(rows), LANES), jnp.float32))
    stacked = jnp.concatenate(rows, axis=0)
    left = lax.broadcasted_iota(jnp.int32, (LANES, LANES), 0) // width
    right = lax.broadcasted_iota(jnp.int32, (LANES, LANES), 1) // width
    same = jnp.where(left == right, 1.0, 0.0).astype(jnp.float32)
    return jnp.dot(
        stacked, same, precision=lax.Precision.HIGHEST, preferred_element_type=jnp.float32
    )


def half_affine(stats, chans, count, gain, shift):
    chunks = chans // LANES
    sums = jnp.concatenate([stats[i : i + 1] for i in range(chunks)], axis=1)
    squares = jnp.concatenate([stats[chunks + i : chunks + i + 1] for i in range(chunks)], axis=1)
    mean = sums / count
    variance = squares / count - mean * mean
    scale = lax.rsqrt(variance + EPSILON) * gain
    return 0.5 * scale, 0.5 * (shift - mean * scale)


def silu_of_half(half):
    return half + half * jnp.tanh(half)


def kernel(
    sizes,
    lat_ref,
    order_ref,
    w_in_ref,
    gain_in_ref,
    shift_in_ref,
    w_mid_ref,
    gain_mid_ref,
    shift_mid_ref,
    w_out_ref,
    blend_ref,
    out_ref,
    lat,
    win,
    gains,
    shifts,
    mid,
    taps,
    first,
    hid,
    acc,
    place,
    stat_out,
    stat_in,
    col_out,
    col_in,
    local_sem,
    lat_s,
    lat_r,
    core_s,
    core_r,
    win_s,
    win_r,
    wcore_s,
    wcore_r,
    gain_s,
    gain_r,
    shift_s,
    shift_r,
    stat_s,
    stat_r,
    col_s,
    col_r,
):
    tiles, chan_count, cores = sizes
    frames, latent_ch, own = lat_ref.shape
    extra = own - LANES
    total_frames = frames * cores
    depth_taps, _, out_ch = w_in_ref.shape
    chans = out_ch * chan_count
    width = chans // GROUPS
    pixels = TSIDE * TSIDE
    tile_rows = tiles // GRID_X
    tile = lax.axis_index("tile")
    chan = lax.axis_index("chan")
    tm = lax.axis_index("tm")
    other = cores - 1 - tm
    split = depth_taps // 2
    parts = ((0, split), (split, depth_taps - split))

    def remote(src, dst, send, recv, device):
        return pltpu.make_async_remote_copy(
            src_ref=src,
            dst_ref=dst,
            send_sem=send,
            recv_sem=recv,
            device_id=device,
            device_id_type=MESH,
        )

    barrier = pltpu.get_barrier_semaphore()
    for far in range(tiles):
        for side in range(chan_count):
            if far or side:
                pl.semaphore_signal(
                    barrier,
                    inc=1,
                    device_id={
                        "tile": lax.rem(tile + far, tiles),
                        "chan": lax.rem(chan + side, chan_count),
                    },
                    device_id_type=MESH,
                )
    pl.semaphore_signal(barrier, inc=1, device_id={"tm": other}, device_id_type=MESH)

    own_win = pltpu.make_async_copy(w_in_ref, win.at[chan], local_sem.at[0])
    own_win.start()
    own_mid = pltpu.make_async_copy(w_mid_ref, mid, local_sem.at[1])
    own_mid.start()

    tail = jnp.zeros((latent_ch, LANES), jnp.float32)
    pixel = lax.broadcasted_iota(jnp.int32, (own, LANES), 0)
    lane = lax.broadcasted_iota(jnp.int32, (own, LANES), 1)
    for f in range(frames):
        lat[tm, tile, f] = lat_ref[f, :, 0:LANES]
        pick = (pixel >= LANES) & (lane == pixel - LANES + extra * f)
        tail = tail + jnp.dot(
            lat_ref[f],
            jnp.where(pick, 1.0, 0.0).astype(jnp.bfloat16),
            preferred_element_type=jnp.float32,
        )
    lat[tm, tile, frames] = tail.astype(jnp.bfloat16)
    blocks = [(down, across) for down in range(min(2, tile_rows)) for across in range(2)]
    for i, (down, across) in enumerate(blocks):
        place[i] = place_matrix(down, across, jnp.bfloat16)
    taps[0:2] = jnp.zeros((2,) + taps.shape[1:], taps.dtype)
    edge = jnp.zeros((TSIDE, hid.shape[2]), hid.dtype)
    for s in range(frames + 2):
        hid[s, 0:TSIDE] = edge
        hid[s, TSIDE + pixels : 2 * TSIDE + pixels] = edge
    col_out[...] = jnp.zeros_like(col_out)

    pl.semaphore_wait(barrier, tiles * chan_count)

    mine = lat.at[tm, tile]
    sends = []
    for t, (start, size) in enumerate(parts):

        @pl.when(tm == t)
        def _():
            for d in range(1, chan_count):
                remote(
                    w_in_ref.at[pl.ds(start, size)],
                    win.at[chan, pl.ds(start, size)],
                    win_s.at[d],
                    win_r.at[d],
                    {"chan": lax.rem(chan + d, chan_count)},
                ).start()

    for d in range(1, tiles):
        copy = remote(
            mine, mine, lat_s.at[d], lat_r.at[d], {"tile": lax.rem(tile + d, tiles)}
        )
        copy.start()
        sends.append(copy)
    copy = remote(mine, mine, core_s.at[0], core_r.at[0], {"tm": other})
    copy.start()
    sends.append(copy)
    for d in range(1, chan_count):
        to = {"chan": lax.rem(chan + d, chan_count)}
        for src, dst, send, recv in (
            (gain_in_ref, gains, gain_s, gain_r),
            (shift_in_ref, shifts, shift_s, shift_r),
        ):
            copy = remote(src, dst.at[chan], send.at[d], recv.at[d], to)
            copy.start()
            sends.append(copy)
    gains[chan] = gain_in_ref[...]
    shifts[chan] = shift_in_ref[...]

    for d in range(1, tiles):
        slot = lat.at[tm, lax.rem(tile - d + tiles, tiles)]
        remote(slot, slot, lat_s.at[d], lat_r.at[d], {"tm": other}).wait_recv()
        copy = remote(slot, slot, core_s.at[d], core_r.at[d], {"tm": other})
        copy.start()
        sends.append(copy)
    for t, (start, size) in enumerate(parts):

        @pl.when(tm == t)
        def _():
            for d in range(1, chan_count):
                slot = win.at[lax.rem(chan - d + chan_count, chan_count), pl.ds(start, size)]
                remote(slot, slot, win_s.at[d], win_r.at[d], {"tm": other}).wait_recv()
                remote(slot, slot, wcore_s.at[d], wcore_r.at[d], {"tm": other}).start()

    for d in range(tiles):
        slot = lat.at[other, lax.rem(tile - d + tiles, tiles)]
        remote(slot, slot, core_s.at[d], core_r.at[d], {"tm": other}).wait_recv()

    window = jnp.zeros((total_frames * latent_ch, pixels), jnp.float32)
    for i, (down, across) in enumerate(blocks):
        block = tile + GRID_X * down + across
        held = jnp.int32(0)
        for d in range(tiles):
            held = jnp.where(order_ref[d] == block, d, held)
        valid = (lax.rem(tile, GRID_X) + across < GRID_X) & (tile // GRID_X + down < tile_rows)
        rows = []
        for t in range(cores):
            message = lat[t, held].astype(jnp.float32)
            for f in range(frames):
                rest = message[frames]
                if f:
                    rest = pltpu.roll(rest, LANES - extra * f, 1)
                rows.append(jnp.concatenate([message[f], rest], axis=1))
        image = jnp.where(valid, jnp.concatenate(rows, axis=0), 0.0).astype(jnp.bfloat16)
        window = window + jnp.dot(image, place[i], preferred_element_type=jnp.float32)
    slot_id = lax.broadcasted_iota(jnp.int32, window.shape, 1)
    row, col = slot_id // TSIDE, slot_id % TSIDE
    for down in range(3):
        for across in range(3):
            offset = (down - 1) * TSIDE + across - 1
            moved = window if offset == 0 else pltpu.roll(window, -offset % pixels, 1)
            inside = (
                (row + down >= 1)
                & (row + down <= TSIDE)
                & (col + across >= 1)
                & (col + across <= TSIDE)
            )
            moved = jnp.where(inside, moved, 0.0).astype(jnp.bfloat16)
            at = (3 * down + across) * latent_ch
            taps[2 : 2 + total_frames, at : at + latent_ch, :] = moved.reshape(
                total_frames, latent_ch, pixels
            )

    own_win.wait()
    for t, (start, size) in enumerate(parts):

        @pl.when(tm != t)
        def _():
            for d in range(1, chan_count):
                slot = win.at[lax.rem(chan - d + chan_count, chan_count), pl.ds(start, size)]
                remote(slot, slot, wcore_s.at[d], wcore_r.at[d], {"tm": other}).wait_recv()

    def first_step(f, carry):
        patch = taps[pl.ds(f, 3)].reshape(depth_taps * latent_ch, pixels)
        sums, squares = [], []
        for c in range(chan_count):
            value = lax.dot_general(
                patch,
                win[c].reshape(depth_taps * latent_ch, out_ch),
                (((0,), (0,)), ((), ())),
                preferred_element_type=jnp.float32,
            )
            first[f, :, out_ch * c : out_ch * (c + 1)] = value
            folded = value.reshape(pixels // 8, 8, out_ch)
            sums.append(jnp.sum(folded, axis=0))
            squares.append(jnp.sum(folded * folded, axis=0))
        return (
            carry[0] + jnp.concatenate(sums, axis=1),
            carry[1] + jnp.concatenate(squares, axis=1),
        )

    zero = jnp.zeros((8, chans), jnp.float32)
    sums, squares = lax.fori_loop(0, total_frames, first_step, (zero, zero))
    for d in range(1, chan_count):
        slot_chan = lax.rem(chan - d + chan_count, chan_count)
        for dst, send, recv in ((gains, gain_s, gain_r), (shifts, shift_s, shift_r)):
            slot = dst.at[slot_chan]
            remote(slot, slot, send.at[d], recv.at[d], {"tm": other}).wait_recv()
    count = total_frames * width * pixels
    stats = group_sums(
        jnp.sum(sums, axis=0, keepdims=True), jnp.sum(squares, axis=0, keepdims=True), width
    )
    scale, offset = half_affine(
        stats,
        chans,
        count,
        jnp.concatenate([gains[c] for c in range(chan_count)], axis=1),
        jnp.concatenate([shifts[c] for c in range(chan_count)], axis=1),
    )

    step_rows = 2 * TSIDE
    col = lax.broadcasted_iota(jnp.int32, (step_rows, chans), 0) % TSIDE

    def hidden_step(s, _):
        frame = frames * tm - 2 + s
        known = frame >= 0
        frame = jnp.maximum(frame, 0)
        for r in range(pixels // step_rows):
            value = silu_of_half(
                first[frame, step_rows * r : step_rows * (r + 1), :] * scale + offset
            )
            value = jnp.where(known, value, 0.0)
            before = jnp.where(col == 0, 0.0, pltpu.roll(value, 1, 0))
            after = jnp.where(col == TSIDE - 1, 0.0, pltpu.roll(value, step_rows - 1, 0))
            for e, piece in enumerate((before, value, after)):
                hid[
                    s,
                    TSIDE + step_rows * r : TSIDE + step_rows * (r + 1),
                    chans * e : chans * (e + 1),
                ] = piece.astype(jnp.bfloat16)
        return 0

    lax.fori_loop(0, frames + 2, hidden_step, 0)
    own_mid.wait()

    batch = 2 if frames % 2 == 0 else 1

    def second_step(g, carry):
        total = None
        for a in range(3):
            for b in range(3):
                value = jnp.dot(
                    hid[pl.ds(batch * g + a, batch), TSIDE * b : TSIDE * b + pixels, :].reshape(
                        batch * pixels, 3 * chans
                    ),
                    mid[9 * a + 3 * b : 9 * a + 3 * b + 3].reshape(3 * chans, out_ch),
                    preferred_element_type=jnp.float32,
                )
                total = value if total is None else total + value
        acc[pl.ds(batch * g, batch)] = total.reshape(batch, pixels, out_ch)
        folded = total.reshape(batch * pixels // 8, 8, out_ch)
        return (
            carry[0] + jnp.sum(folded, axis=0),
            carry[1] + jnp.sum(folded * folded, axis=0),
        )

    zero = jnp.zeros((8, out_ch), jnp.float32)
    sums, squares = lax.fori_loop(0, frames // batch, second_step, (zero, zero))
    stats = group_sums(
        jnp.sum(sums, axis=0, keepdims=True), jnp.sum(squares, axis=0, keepdims=True), width
    )
    stat_out[...] = stats
    stat_copy = remote(stat_out, stat_in, stat_s, stat_r, {"tm": other})
    stat_copy.start()
    stat_copy.wait()
    stats = stats + stat_in[...]
    scale, offset = half_affine(stats, out_ch, count, gain_mid_ref[...], shift_mid_ref[...])
    colors = out_ref.shape[1]
    for f in range(frames):
        upper = silu_of_half(acc[f] * scale + offset).astype(jnp.bfloat16)
        col_out[colors * f : colors * (f + 1), :] = lax.dot_general(
            w_out_ref[...], upper, (((1,), (1,)), ((), ())), preferred_element_type=jnp.float32
        )

    def tile_valid_to(down, across):
        return (lax.rem(tile, GRID_X) + across < GRID_X) & (tile // GRID_X + down < tile_rows)

    def tile_valid_from(down, across):
        return (lax.rem(tile, GRID_X) >= across) & (tile // GRID_X >= down)

    def color_copy(i, d, hop):
        return remote(
            col_out,
            col_in.at[i, d],
            col_s.at[i, d],
            col_r.at[i, d],
            {
                "tile": lax.rem(tile + hop, tiles),
                "chan": lax.rem(chan + d, chan_count),
            },
        )

    for i, (down, across) in reversed(list(enumerate(blocks))):
        for d in reversed(range(chan_count)):
            if i or d:
                pl.when(tile_valid_to(down, across))(
                    color_copy(i, d, GRID_X * down + across).start
                )

    rows = col_out.shape[0]
    row_id = lax.broadcasted_iota(jnp.int32, (rows, pixels), 0)
    blended = jnp.zeros((rows, 2 * LANES), jnp.float32)
    for i, (down, across) in enumerate(blocks):
        hop = GRID_X * down + across
        here = tile_valid_from(down, across)
        for d in range(chan_count):
            if i or d:
                pl.when(here)(color_copy(i, d, hop).wait_recv)
        color = col_out[...] if i == 0 else col_in[i, 0]
        for d in range(1, chan_count):
            color = color + col_in[i, d]
        weight = blend_ref[pl.ds(lax.rem(tile - hop + tiles, tiles), 1), :]
        color = jnp.where(row_id == colors * frames, 1.0, color) * weight
        color = jnp.where(here, color, 0.0)
        blended = blended + lax.dot_general(
            color,
            place[i].astype(jnp.float32),
            (((1,), (1,)), ((), ())),
            precision=lax.Precision.HIGHEST,
            preferred_element_type=jnp.float32,
        )
    result = blended / blended[colors * frames : colors * frames + 1]
    for f in range(frames):
        out_ref[f] = result[colors * f : colors * (f + 1), :own]

    for copy in sends:
        copy.wait_send()
    for t, (start, size) in enumerate(parts):

        @pl.when(tm == t)
        def _():
            for d in range(1, chan_count):
                slot = win.at[lax.rem(chan - d + chan_count, chan_count), pl.ds(start, size)]
                remote(slot, slot, win_s.at[d], win_r.at[d], {"tm": other}).wait_send()
                remote(slot, slot, wcore_s.at[d], wcore_r.at[d], {"tm": other}).wait_send()

    for i, (down, across) in enumerate(blocks):
        for d in range(chan_count):
            if i or d:
                pl.when(tile_valid_to(down, across))(
                    color_copy(i, d, GRID_X * down + across).wait_send
                )


def body(
    sizes,
    latents,
    tile_order,
    w_in,
    gain_in,
    shift_in,
    w_mid,
    gain_mid,
    shift_mid,
    w_out,
    blend_weight,
):
    tiles, chan_count, cores = sizes
    frames, latent_ch, own = latents.shape
    depth_taps, chans, out_ch = w_mid.shape
    total_frames = frames * cores
    pixels = TSIDE * TSIDE
    colors = w_out.shape[0]
    vmem = pl.BlockSpec(memory_space=pltpu.VMEM)
    anywhere = pl.BlockSpec(memory_space=pl.ANY)
    bf16, f32 = jnp.bfloat16, jnp.float32
    block_count = 2 * min(2, tiles // GRID_X)
    color_rows = -(-(colors * frames + 1) // 8) * 8
    dma = pltpu.SemaphoreType.DMA
    scratch = [
        pltpu.VMEM((cores, tiles, frames + 1, latent_ch, LANES), bf16),
        pltpu.VMEM((chan_count, depth_taps, latent_ch, out_ch), bf16),
        pltpu.VMEM((chan_count, 1, out_ch), f32),
        pltpu.VMEM((chan_count, 1, out_ch), f32),
        pltpu.VMEM((depth_taps, chans, out_ch), bf16),
        pltpu.VMEM((total_frames + 2, 9 * latent_ch, pixels), bf16),
        pltpu.VMEM((total_frames, pixels, chans), f32),
        pltpu.VMEM((frames + 2, pixels + 2 * TSIDE, 3 * chans), bf16),
        pltpu.VMEM((frames, pixels, out_ch), f32),
        pltpu.VMEM((block_count, 2 * LANES, pixels), bf16),
        pltpu.VMEM((8, LANES), f32),
        pltpu.VMEM((8, LANES), f32),
        pltpu.VMEM((color_rows, pixels), f32),
        pltpu.VMEM((block_count, chan_count, color_rows, pixels), f32),
        dma((2,)),
        dma((tiles,)),
        dma((tiles,)),
        dma((tiles,)),
        dma((tiles,)),
    ]
    scratch += [dma((chan_count,)) for _ in range(8)]
    scratch += [dma, dma, dma((block_count, chan_count)), dma((block_count, chan_count))]
    return pl.pallas_call(
        functools.partial(kernel, sizes),
        out_shape=jax.ShapeDtypeStruct((frames, colors, own), f32),
        in_specs=[
            vmem,
            pl.BlockSpec(memory_space=pltpu.SMEM),
            anywhere,
            vmem,
            vmem,
            anywhere,
            vmem,
            vmem,
            vmem,
            vmem,
        ],
        out_specs=vmem,
        scratch_shapes=scratch,
        compiler_params=pltpu.CompilerParams(collective_id=0, has_side_effects=True),
    )(
        latents,
        tile_order,
        w_in,
        gain_in.reshape(1, -1),
        shift_in.reshape(1, -1),
        w_mid,
        gain_mid.reshape(1, -1),
        shift_mid.reshape(1, -1),
        w_out,
        blend_weight,
    )


def solution(mesh):
    placed = (
        P("tm", "groups", "tile"),
        P("groups"),
        P(None, None, "chan"),
        P("chan"),
        P("chan"),
        P(None, None, "chan"),
        P("chan"),
        P("chan"),
        P(None, "chan"),
        P("groups", None),
    )
    sizes = (mesh.shape["tile"], mesh.shape["chan"], mesh.shape["tm"])
    return jax.shard_map(
        functools.partial(body, sizes),
        mesh=mesh,
        in_specs=placed,
        out_specs=P("tm", "groups", "tile"),
        check_vma=False,
    )
```

time: 142 us -> 31.3 us (0.22)
  matrix products: 33.9 us -> 0 us
  blocking collectives: 30.3 us -> 0 us
  Pallas kernels: 0 us -> 29.7 us
  waiting for transfers between devices: 23 us -> 0 us
  other arithmetic: 14.9 us -> 0 us
  between operations: 14.3 us -> 0.01 us
  starting transfers between devices: 13.2 us -> 0 us
  local copies, waits for them, and re-layouts: 12.1 us -> 1.32 us
    dot_general x55 -> x0, matrix products: 33.9 us -> none  [the longest x54 33.5 us: causal_conv(): jnp.einsum('fcp,co->fop', moved, weights[9 * depth + 3 * down + across],...]
    pallas_call x0 -> x1, Pallas kernels: none -> 29.7 us  [body(): pl.pallas_call(functools.partial(kernel, sizes), out_shape=jax.ShapeDtype...]
    all_gather x1 -> x0, waiting for transfers between devices: 21.1 us -> none  [body(): lax.all_gather(with_history(hidden), 'chan', axis=1, tiled=True)]
    all_gather x1 -> x0, blocking collectives: 18.3 us -> none  [body(): whole = lax.all_gather(latents, 'tile', axis=2, tiled=True)]
    ppermute x8 -> x0, starting transfers between devices: 13.2 us -> none  [shifted(): lax.ppermute(value, axis, [(source, source + steps) for source in range(l...]
    psum x3 -> x0, blocking collectives: 12.1 us -> none  [the longest x1 7.13 us: body(): numer = lax.psum(numer, 'chan')]
    scatter-add x2 -> x0, other arithmetic: 10.8 us -> none  [the longest x1 8.52 us: spread(): numer = jnp.zeros((color.shape[0], 3, total_pixels), jnp.float32).at[:, :...]
    slice x10 -> x0, local copies, waits for them, and re-layouts: 6.57 us -> none  [the longest x8 6.55 us: causal_conv(): moved = jnp.roll(window, -offset, axis=2)]
  transfers between devices with their start and end apart: 9 -> 0, of which waited for: 3 -> 0; matrix products, arithmetic and copies ran while one was open for 30% -> 0% of each run, Pallas kernels for 0% -> 0%
where the time goes in v1:
time: 31.3 us; the launch traced here: 31.1 us
  Pallas kernels  29.7 us (95%)
  local copies, waits for them, and re-layouts  1.32 us (4%)
    pallas_call x1, Pallas kernels, body(): pl.pallas_call(functools.partial(kernel, sizes), out_shape=jax.ShapeDtype...  29.7 us
    pallas_call x1, local copies, waits for them, and re-layouts, body(): pl.pallas_call(functools.partial(kernel, sizes), out_shape=jax.ShapeDtype...  1.32 us

profile of v1, /device:TPU:0, one launch (start us, length us, event | category | flops | bytes accessed | tf_op | source)
XLA Modules:
  0.0 31.1 jit_solution(2120675213235071537)
XLA Ops:
  0.0 29.7 %shard_map.100 = f32[4,3,144]{2,1,0:T(4,128)} custom-call(bf16[4,16,144]{2,1,0:T(8,128)(2,1)} %lat_ref.1, s32[4]{0:T(128)} %order_ref.1, bf16[27,16,256]{2,1,0:T(8,128)(2,1)} %w_in_ref.1, f32[1,256]{1,0:T(1,128)} %bitcast.4, f32[1,256]{1,0:T(1,128)} %bitcast.5, bf16[27,512,256]{2,1,0:T(8,128)(2,1)} %w_mid_ref.1, f32[1,256]{1,0:T(1,128)} %bitcast.6, ...), custom_call_target="tpu_custom_call" | custom-call | tf_op jit(solution)/shard_map/pallas_call | solution.py:493
  29.7 1.3 %copy.11 = f32[4,3,144]{2,0,1:T(4,128)} copy(f32[4,3,144]{2,1,0:T(4,128)} %shard_map.100) | data formatting | bytes 13824 | tf_op jit(solution)/shard_map/pallas_call | solution.py:493

commit v2 on v1

--- a/solution.py
+++ b/solution.py
@@ -58,17 +58,24 @@
 
 def kernel(
     sizes,
-    lat_ref,
-    order_ref,
+    lat_hbm,
+    order_hbm,
     w_in_ref,
     gain_in_ref,
     shift_in_ref,
     w_mid_ref,
+    gain_mid_hbm,
+    shift_mid_hbm,
+    w_out_hbm,
+    blend_hbm,
+    out_ref,
+    lat_ref,
+    order_ref,
     gain_mid_ref,
     shift_mid_ref,
     w_out_ref,
     blend_ref,
-    out_ref,
+    first_sums,
     lat,
     win,
     gains,
@@ -102,7 +109,7 @@
     col_r,
 ):
     tiles, chan_count, cores = sizes
-    frames, latent_ch, own = lat_ref.shape
+    frames, latent_ch, own = lat_hbm.shape
     extra = own - LANES
     total_frames = frames * cores
     depth_taps, _, out_ch = w_in_ref.shape
@@ -142,14 +149,32 @@
                 )
     pl.semaphore_signal(barrier, inc=1, device_id={"tm": other}, device_id_type=MESH)
 
-    own_win = pltpu.make_async_copy(w_in_ref, win.at[chan], local_sem.at[0])
-    own_win.start()
-    own_mid = pltpu.make_async_copy(w_mid_ref, mid, local_sem.at[1])
-    own_mid.start()
+    pairs = (
+        (lat_hbm, lat_ref),
+        (order_hbm, order_ref),
+        (w_in_ref, win.at[chan]),
+        (gain_in_ref, gains.at[chan]),
+        (shift_in_ref, shifts.at[chan]),
+        (gain_mid_hbm, gain_mid_ref),
+        (shift_mid_hbm, shift_mid_ref),
+        (w_out_hbm, w_out_ref),
+        (blend_hbm, blend_ref),
+        (w_mid_ref, mid),
+    )
+    loads = [
+        pltpu.make_async_copy(src, dst, local_sem.at[i]) for i, (src, dst) in enumerate(pairs)
+    ]
+    for load in loads:
+        load.start()
+
+    blocks = [(down, across) for down in range(min(2, tile_rows)) for across in range(2)]
+    for i, (down, across) in enumerate(blocks):
+        place[i] = place_matrix(down, across, jnp.bfloat16)
 
     tail = jnp.zeros((latent_ch, LANES), jnp.float32)
     pixel = lax.broadcasted_iota(jnp.int32, (own, LANES), 0)
     lane = lax.broadcasted_iota(jnp.int32, (own, LANES), 1)
+    loads[0].wait()
     for f in range(frames):
         lat[tm, tile, f] = lat_ref[f, :, 0:LANES]
         pick = (pixel >= LANES) & (lane == pixel - LANES + extra * f)
@@ -159,9 +184,6 @@
             preferred_element_type=jnp.float32,
         )
     lat[tm, tile, frames] = tail.astype(jnp.bfloat16)
-    blocks = [(down, across) for down in range(min(2, tile_rows)) for across in range(2)]
-    for i, (down, across) in enumerate(blocks):
-        place[i] = place_matrix(down, across, jnp.bfloat16)
     taps[0:2] = jnp.zeros((2,) + taps.shape[1:], taps.dtype)
     edge = jnp.zeros((TSIDE, hid.shape[2]), hid.dtype)
     for s in range(frames + 2):
@@ -186,7 +208,8 @@
                     {"chan": lax.rem(chan + d, chan_count)},
                 ).start()
 
-    for d in range(1, tiles):
+    for step in range(1, tiles):
+        d = jnp.where(2 * tile < tiles, tiles - step, step)
         copy = remote(
             mine, mine, lat_s.at[d], lat_r.at[d], {"tile": lax.rem(tile + d, tiles)}
         )
@@ -204,8 +227,6 @@
             copy = remote(src, dst.at[chan], send.at[d], recv.at[d], to)
             copy.start()
             sends.append(copy)
-    gains[chan] = gain_in_ref[...]
-    shifts[chan] = shift_in_ref[...]
 
     for d in range(1, tiles):
         slot = lat.at[tm, lax.rem(tile - d + tiles, tiles)]
@@ -226,6 +247,7 @@
         slot = lat.at[other, lax.rem(tile - d + tiles, tiles)]
         remote(slot, slot, core_s.at[d], core_r.at[d], {"tm": other}).wait_recv()
 
+    loads[1].wait()
     window = jnp.zeros((total_frames * latent_ch, pixels), jnp.float32)
     for i, (down, across) in enumerate(blocks):
         block = tile + GRID_X * down + across
@@ -261,36 +283,38 @@
                 total_frames, latent_ch, pixels
             )
 
-    own_win.wait()
-    for t, (start, size) in enumerate(parts):
-
-        @pl.when(tm != t)
-        def _():
-            for d in range(1, chan_count):
-                slot = win.at[lax.rem(chan - d + chan_count, chan_count), pl.ds(start, size)]
-                remote(slot, slot, wcore_s.at[d], wcore_r.at[d], {"tm": other}).wait_recv()
-
-    def first_step(f, carry):
-        patch = taps[pl.ds(f, 3)].reshape(depth_taps * latent_ch, pixels)
-        sums, squares = [], []
-        for c in range(chan_count):
-            value = lax.dot_general(
-                patch,
-                win[c].reshape(depth_taps * latent_ch, out_ch),
-                (((0,), (0,)), ((), ())),
-                preferred_element_type=jnp.float32,
-            )
-            first[f, :, out_ch * c : out_ch * (c + 1)] = value
-            folded = value.reshape(pixels // 8, 8, out_ch)
-            sums.append(jnp.sum(folded, axis=0))
-            squares.append(jnp.sum(folded * folded, axis=0))
-        return (
-            carry[0] + jnp.concatenate(sums, axis=1),
-            carry[1] + jnp.concatenate(squares, axis=1),
-        )
-
-    zero = jnp.zeros((8, chans), jnp.float32)
-    sums, squares = lax.fori_loop(0, total_frames, first_step, (zero, zero))
+    loads[2].wait()
+    zero = jnp.zeros((8, out_ch), jnp.float32)
+    for d in range(chan_count):
+        source = lax.rem(chan - d + chan_count, chan_count)
+        if d:
+            for t, (start, size) in enumerate(parts):
+
+                @pl.when(tm != t)
+                def _():
+                    slot = win.at[source, pl.ds(start, size)]
+                    remote(slot, slot, wcore_s.at[d], wcore_r.at[d], {"tm": other}).wait_recv()
+
+        def first_step(g, carry):
+            sums, squares = carry
+            for f in (2 * g, 2 * g + 1):
+                value = lax.dot_general(
+                    taps[pl.ds(f, 3)].reshape(depth_taps * latent_ch, pixels),
+                    win[source].reshape(depth_taps * latent_ch, out_ch),
+                    (((0,), (0,)), ((), ())),
+                    preferred_element_type=jnp.float32,
+                )
+                first[source, f] = value
+                folded = value.reshape(pixels // 8, 8, out_ch)
+                sums = sums + jnp.sum(folded, axis=0)
+                squares = squares + jnp.sum(folded * folded, axis=0)
+            return sums, squares
+
+        sums, squares = lax.fori_loop(0, total_frames // 2, first_step, (zero, zero))
+        first_sums[source, 0:1] = jnp.sum(sums, axis=0, keepdims=True)
+        first_sums[source, 1:2] = jnp.sum(squares, axis=0, keepdims=True)
+    for load in loads[3:9]:
+        load.wait()
     for d in range(1, chan_count):
         slot_chan = lax.rem(chan - d + chan_count, chan_count)
         for dst, send, recv in ((gains, gain_s, gain_r), (shifts, shift_s, shift_r)):
@@ -298,7 +322,9 @@
             remote(slot, slot, send.at[d], recv.at[d], {"tm": other}).wait_recv()
     count = total_frames * width * pixels
     stats = group_sums(
-        jnp.sum(sums, axis=0, keepdims=True), jnp.sum(squares, axis=0, keepdims=True), width
+        jnp.concatenate([first_sums[c, 0:1] for c in range(chan_count)], axis=1),
+        jnp.concatenate([first_sums[c, 1:2] for c in range(chan_count)], axis=1),
+        width,
     )
     scale, offset = half_affine(
         stats,
@@ -309,15 +335,18 @@
     )
 
     step_rows = 2 * TSIDE
-    col = lax.broadcasted_iota(jnp.int32, (step_rows, chans), 0) % TSIDE
-
-    def hidden_step(s, _):
+    steps = pixels // step_rows
+    col = lax.broadcasted_iota(jnp.int32, (step_rows, out_ch), 0) % TSIDE
+
+    def hidden_rows(s, r):
         frame = frames * tm - 2 + s
         known = frame >= 0
         frame = jnp.maximum(frame, 0)
-        for r in range(pixels // step_rows):
+        for c in range(chan_count):
+            channels = slice(out_ch * c, out_ch * (c + 1))
             value = silu_of_half(
-                first[frame, step_rows * r : step_rows * (r + 1), :] * scale + offset
+                first[c, frame, step_rows * r : step_rows * (r + 1), :] * scale[:, channels]
+                + offset[:, channels]
             )
             value = jnp.where(known, value, 0.0)
             before = jnp.where(col == 0, 0.0, pltpu.roll(value, 1, 0))
@@ -326,36 +355,43 @@
                 hid[
                     s,
                     TSIDE + step_rows * r : TSIDE + step_rows * (r + 1),
-                    chans * e : chans * (e + 1),
+                    chans * e + out_ch * c : chans * e + out_ch * (c + 1),
                 ] = piece.astype(jnp.bfloat16)
-        return 0
-
-    lax.fori_loop(0, frames + 2, hidden_step, 0)
-    own_mid.wait()
+
+    def hidden_step(s, carry):
+        for r in range(steps):
+            hidden_rows(s, r)
+        return carry
 
     batch = 2 if frames % 2 == 0 else 1
-
-    def second_step(g, carry):
+    lax.fori_loop(0, batch + 2, hidden_step, 0)
+    loads[9].wait()
+
+    sums = squares = jnp.zeros((8, out_ch), jnp.float32)
+    for at in range(0, frames, batch):
+        ahead = [
+            (s, r)
+            for s in range(at + batch + 2, min(at + 2 * batch, frames) + 2)
+            for r in range(steps)
+        ]
+        share = -(-len(ahead) // 9)
         total = None
         for a in range(3):
             for b in range(3):
                 value = jnp.dot(
-                    hid[pl.ds(batch * g + a, batch), TSIDE * b : TSIDE * b + pixels, :].reshape(
+                    hid[at + a : at + a + batch, TSIDE * b : TSIDE * b + pixels, :].reshape(
                         batch * pixels, 3 * chans
                     ),
                     mid[9 * a + 3 * b : 9 * a + 3 * b + 3].reshape(3 * chans, out_ch),
                     preferred_element_type=jnp.float32,
                 )
                 total = value if total is None else total + value
-        acc[pl.ds(batch * g, batch)] = total.reshape(batch, pixels, out_ch)
+                for s, r in ahead[share * (3 * a + b) : share * (3 * a + b + 1)]:
+                    hidden_rows(s, r)
+        acc[at : at + batch] = total.reshape(batch, pixels, out_ch)
         folded = total.reshape(batch * pixels // 8, 8, out_ch)
-        return (
-            carry[0] + jnp.sum(folded, axis=0),
-            carry[1] + jnp.sum(folded * folded, axis=0),
-        )
-
-    zero = jnp.zeros((8, out_ch), jnp.float32)
-    sums, squares = lax.fori_loop(0, frames // batch, second_step, (zero, zero))
+        sums = sums + jnp.sum(folded, axis=0)
+        squares = squares + jnp.sum(folded * folded, axis=0)
     stats = group_sums(
         jnp.sum(sums, axis=0, keepdims=True), jnp.sum(squares, axis=0, keepdims=True), width
     )
@@ -365,12 +401,14 @@
     stat_copy.wait()
     stats = stats + stat_in[...]
     scale, offset = half_affine(stats, out_ch, count, gain_mid_ref[...], shift_mid_ref[...])
-    colors = out_ref.shape[1]
+    colors = out_ref.shape[0]
     for f in range(frames):
         upper = silu_of_half(acc[f] * scale + offset).astype(jnp.bfloat16)
-        col_out[colors * f : colors * (f + 1), :] = lax.dot_general(
+        color = lax.dot_general(
             w_out_ref[...], upper, (((1,), (1,)), ((), ())), preferred_element_type=jnp.float32
         )
+        for o in range(colors):
+            col_out[frames * o + f : frames * o + f + 1, :] = color[o : o + 1]
 
     def tile_valid_to(down, across):
         return (lax.rem(tile, GRID_X) + across < GRID_X) & (tile // GRID_X + down < tile_rows)
@@ -420,8 +458,8 @@
             preferred_element_type=jnp.float32,
         )
     result = blended / blended[colors * frames : colors * frames + 1]
-    for f in range(frames):
-        out_ref[f] = result[colors * f : colors * (f + 1), :own]
+    for o in range(colors):
+        out_ref[o] = result[frames * o : frames * (o + 1), :own]
 
     for copy in sends:
         copy.wait_send()
@@ -467,14 +505,22 @@
     block_count = 2 * min(2, tiles // GRID_X)
     color_rows = -(-(colors * frames + 1) // 8) * 8
     dma = pltpu.SemaphoreType.DMA
+    smem = pltpu.SMEM
     scratch = [
+        pltpu.VMEM(latents.shape, bf16),
+        smem(tile_order.shape, jnp.int32),
+        pltpu.VMEM((1, out_ch), f32),
+        pltpu.VMEM((1, out_ch), f32),
+        pltpu.VMEM(w_out.shape, bf16),
+        pltpu.VMEM(blend_weight.shape, f32),
+        pltpu.VMEM((chan_count, 8, out_ch), f32),
         pltpu.VMEM((cores, tiles, frames + 1, latent_ch, LANES), bf16),
         pltpu.VMEM((chan_count, depth_taps, latent_ch, out_ch), bf16),
         pltpu.VMEM((chan_count, 1, out_ch), f32),
         pltpu.VMEM((chan_count, 1, out_ch), f32),
         pltpu.VMEM((depth_taps, chans, out_ch), bf16),
         pltpu.VMEM((total_frames + 2, 9 * latent_ch, pixels), bf16),
-        pltpu.VMEM((total_frames, pixels, chans), f32),
+        pltpu.VMEM((chan_count, total_frames, pixels, out_ch), f32),
         pltpu.VMEM((frames + 2, pixels + 2 * TSIDE, 3 * chans), bf16),
         pltpu.VMEM((frames, pixels, out_ch), f32),
         pltpu.VMEM((block_count, 2 * LANES, pixels), bf16),
@@ -482,7 +528,7 @@
         pltpu.VMEM((8, LANES), f32),
         pltpu.VMEM((color_rows, pixels), f32),
         pltpu.VMEM((block_count, chan_count, color_rows, pixels), f32),
-        dma((2,)),
+        dma((10,)),
         dma((tiles,)),
         dma((tiles,)),
         dma((tiles,)),
@@ -490,21 +536,10 @@
     ]
     scratch += [dma((chan_count,)) for _ in range(8)]
     scratch += [dma, dma, dma((block_count, chan_count)), dma((block_count, chan_count))]
-    return pl.pallas_call(
+    colored = pl.pallas_call(
         functools.partial(kernel, sizes),
-        out_shape=jax.ShapeDtypeStruct((frames, colors, own), f32),
-        in_specs=[
-            vmem,
-            pl.BlockSpec(memory_space=pltpu.SMEM),
-            anywhere,
-            vmem,
-            vmem,
-            anywhere,
-            vmem,
-            vmem,
-            vmem,
-            vmem,
-        ],
+        out_shape=jax.ShapeDtypeStruct((colors, frames, own), f32),
+        in_specs=[anywhere] * 10,
         out_specs=vmem,
         scratch_shapes=scratch,
         compiler_params=pltpu.CompilerParams(collective_id=0, has_side_effects=True),
@@ -520,6 +555,7 @@
         w_out,
         blend_weight,
     )
+    return jnp.transpose(colored, (1, 0, 2))
 
 
 def solution(mesh):

time: 31.3 us -> 30 us (0.958)
  Pallas kernels: 29.7 us -> 28.4 us
    pallas_call x1 -> x0, local copies, waits for them, and re-layouts: 1.32 us -> none  [body(): pl.pallas_call(functools.partial(kernel, sizes), out_shape=jax.ShapeDtype...]
    unnamed x0 -> x1, local copies, waits for them, and re-layouts: none -> 1.31 us
    pallas_call x1, Pallas kernels: 29.7 us -> 28.4 us  [body(): pl.pallas_call(functools.partial(kernel, sizes), out_shape=jax.ShapeDtype...]
where the time goes in v2:
time: 30 us; the launch traced here: 29.8 us
  Pallas kernels  28.4 us (95%)
  local copies, waits for them, and re-layouts  1.31 us (4%)
    pallas_call x1, Pallas kernels, body(): pl.pallas_call(functools.partial(kernel, sizes), out_shape=jax.ShapeDtype...  28.4 us
    unnamed x1, local copies, waits for them, and re-layouts  1.31 us

profile of v2, /device:TPU:0, one launch (start us, length us, event | category | flops | bytes accessed | tf_op | source)
XLA Modules:
  0.0 29.8 jit_solution(7653032563869609768)
XLA Ops:
  0.0 28.4 %shard_map.100 = f32[3,4,144]{2,1,0:T(4,128)} custom-call(bf16[4,16,144]{2,1,0:T(8,128)(2,1)} %lat_hbm.1, s32[4]{0:T(128)} %order_hbm.1, bf16[27,16,256]{2,1,0:T(8,128)(2,1)} %w_in_ref.1, f32[1,256]{1,0:T(1,128)} %bitcast.6, f32[1,256]{1,0:T(1,128)} %bitcast.7, bf16[27,512,256]{2,1,0:T(8,128)(2,1)} %w_mid_ref.1, f32[1,256]{1,0:T(1,128)} %bitcast.8, ...), custom_call_target="tpu_custom_call" | custom-call | tf_op jit(solution)/shard_map/pallas_call | solution.py:539
  28.5 1.3 %copy.12 = f32[4,3,144]{2,0,1:T(4,128)} copy(f32[4,3,144]{2,0,1:T(4,128)} %bitcast.5) | data formatting | bytes 13824

commit v3 on v2

--- a/solution.py
+++ b/solution.py
@@ -164,7 +164,7 @@
     loads = [
         pltpu.make_async_copy(src, dst, local_sem.at[i]) for i, (src, dst) in enumerate(pairs)
     ]
-    for load in loads:
+    for load in loads[:9]:
         load.start()
 
     blocks = [(down, across) for down in range(min(2, tile_rows)) for across in range(2)]
@@ -228,6 +228,7 @@
             copy.start()
             sends.append(copy)
 
+    loads[9].start()
     for d in range(1, tiles):
         slot = lat.at[tm, lax.rem(tile - d + tiles, tiles)]
         remote(slot, slot, lat_s.at[d], lat_r.at[d], {"tm": other}).wait_recv()

time: 30 us -> 30 us (level)
  no operation moved by 1% of the time
where the time goes in v3:
time: 30 us; the launch traced here: 29.8 us
  Pallas kernels  28.4 us (95%)
  local copies, waits for them, and re-layouts  1.31 us (4%)
    pallas_call x1, Pallas kernels, body(): pl.pallas_call(functools.partial(kernel, sizes), out_shape=jax.ShapeDtype...  28.4 us
    unnamed x1, local copies, waits for them, and re-layouts  1.31 us

profile of v3, /device:TPU:0, one launch (start us, length us, event | category | flops | bytes accessed | tf_op | source)
XLA Modules:
  0.0 29.8 jit_solution(9441744855955045633)
XLA Ops:
  0.0 28.4 %shard_map.100 = f32[3,4,144]{2,1,0:T(4,128)} custom-call(bf16[4,16,144]{2,1,0:T(8,128)(2,1)} %lat_hbm.1, s32[4]{0:T(128)} %order_hbm.1, bf16[27,16,256]{2,1,0:T(8,128)(2,1)} %w_in_ref.1, f32[1,256]{1,0:T(1,128)} %bitcast.6, f32[1,256]{1,0:T(1,128)} %bitcast.7, bf16[27,512,256]{2,1,0:T(8,128)(2,1)} %w_mid_ref.1, f32[1,256]{1,0:T(1,128)} %bitcast.8, ...), custom_call_target="tpu_custom_call" | custom-call | tf_op jit(solution)/shard_map/pallas_call | solution.py:540
  28.5 1.3 %copy.12 = f32[4,3,144]{2,0,1:T(4,128)} copy(f32[4,3,144]{2,0,1:T(4,128)} %bitcast.5) | data formatting | bytes 13824
